TPU v7x, 512 devices: a whole 4x8x8 slice. The times are simulated.
512 devices in a mesh: row: 64 (over y, x, core), col: 8 (over z).
Axes of the slice: x: 4, y: 8, z: 8, core: 2. Of those that a mesh axis runs over, the one named last changes fastest.
Arguments:
- hamiltonian: float32 [24576, 24576], P('row', 'col'), as said below
- previous: float32 [24576, 56], P('row', 'col'), may hold values from -6 to 6
- correlation_map: int32 [24576], P('row'), may hold values from 0 to 24575, each once
- lower_cut: float32 [1], replicated, may hold values from 0.5 to 1.5
- upper_bound: float32 [1], replicated, may hold values from 5.5 to 6.5
Outputs:
- basis_out: float32 [24576, 56], P('row', 'col')
- ritz_matrix: float32 [56, 56], replicated
Inputs may be any that keep to these rules, and one draw needn't show every extreme that they name: correlation_map names every index of 0 .. 24575 exactly once. hamiltonian is symmetric.
All inputs are finite; a program needn't handle non-finite values.
Results may differ from a plain program's by a relative error of at most 0.00013.
Values sent between devices are 32-bit elements; how exact they have to be, the bound alone decides.
A program may use at most 64 MiB of HBM per device.

v0:
```python
import jax
import jax.numpy as jnp
from jax import lax
from jax.sharding import PartitionSpec as P

N = 24576
DEG = 4


def body(hamiltonian, previous, correlation_map, lower_cut, upper_bound):
    column_groups = lax.axis_size("col")
    group_width = previous.shape[1]
    width = group_width * column_groups
    centre = (upper_bound[0] + lower_cut[0]) * 0.5
    half_width = (upper_bound[0] - lower_cut[0]) * 0.5
    spread = lax.all_gather(previous, "row", axis=0, tiled=True)
    start_block = jnp.take(spread, correlation_map, axis=0)

    def operate_on(vectors):
        spread_rows = lax.all_gather(vectors, "row", axis=0, tiled=True)
        wanted = lax.all_to_all(spread_rows, "col", split_axis=0, concat_axis=1, tiled=True)
        partial_sum = jnp.dot(hamiltonian, wanted, precision=lax.Precision.HIGHEST)
        return lax.psum_scatter(partial_sum, "col", scatter_dimension=1, tiled=True)

    earlier = start_block
    current = (operate_on(earlier) - centre * earlier) / half_width
    for repeat in range(DEG - 1):
        following = 2.0 * (operate_on(current) - centre * current) / half_width - earlier
        earlier = current
        current = following
    column_index = lax.axis_index("col")
    full_rows = lax.all_gather(current, "col", axis=1, tiled=True)
    empty = jnp.zeros((width, width), jnp.float32)
    block_rows = jnp.dot(current.T, full_rows, precision=lax.Precision.HIGHEST)
    gram_part = lax.dynamic_update_slice_in_dim(empty, block_rows, column_index * group_width, 0)
    gram_total = lax.psum(gram_part, ("row", "col"))
    applied = operate_on(current)
    block_cols = jnp.dot(full_rows.T, applied, precision=lax.Precision.HIGHEST)
    proj_total = lax.psum(
        lax.dynamic_update_slice_in_dim(empty, block_cols, column_index * group_width, 1),
        ("row", "col"),
    )
    gram_matrix = gram_total / N
    projected = proj_total / N
    factor = jnp.linalg.cholesky(gram_matrix)
    identity = jnp.eye(width, dtype=jnp.float32)
    inverse = lax.linalg.triangular_solve(factor, identity, left_side=True, lower=True)
    own_columns = lax.dynamic_slice_in_dim(inverse.T, column_index * group_width, group_width, 1)
    basis_out = jnp.dot(full_rows, own_columns, precision=lax.Precision.HIGHEST)
    ritz_matrix = jnp.dot(
        jnp.dot(inverse, projected, precision=lax.Precision.HIGHEST),
        inverse.T,
        precision=lax.Precision.HIGHEST,
    )
    return (basis_out, ritz_matrix)


def solution(mesh):
    return jax.shard_map(
        body,
        mesh=mesh,
        in_specs=(P("row", "col"), P("row", "col"), P("row"), P(), P()),
        out_specs=(P("row", "col"), P()),
        check_vma=False,
    )
```

profile of v0, /device:TPU:1, one launch (start us, length us, event | category | flops | bytes accessed | tf_op | source)
XLA Modules:
  0.0 1014.7 jit_solution(17210025577529272954)
XLA Ops:
  9.4 70.1 %all_gather.21 = f32[24576,7]{1,0:T(8,128)} all-gather(f32[384,7]{1,0:T(8,128)S(1)} %copy.41), channel_id=1, replica_groups=mesh['row'=64,'col'=8] {'row'}, dimensions={0}, use_global_device_ids=true | all-gather | bytes 698880 | tf_op jit(solution)/shard_map/all_gather | solution.py:16
  79.6 5.7 gather_fusion
  85.4 48.9 %all_gather.22 = f32[24576,7]{0,1:T(8,128)S(1)} all-gather(f32[384,7]{0,1:T(8,128)S(1)} %broadcast_select_fusion), channel_id=1, replica_groups=mesh['row'=64,'col'=8] {'row'}, dimensions={0}, use_global_device_ids=true | all-gather | bytes 698880 | tf_op jit(solution)/shard_map/all_gather | solution.py:20
  134.3 30.6 %all_to_all.95 = f32[8,3072,7]{1,2,0:T(8,128)S(1)} all-to-all(f32[8,3072,7]{1,2,0:T(8,128)S(1)} %bitcast.63), channel_id=1, replica_groups=mesh['row'=64,'col'=8] {'col'}, dimensions={0} | all-to-all | bytes 1376256 | tf_op jit(solution)/shard_map/all_to_all | solution.py:21
  164.9 7.4 convolution_bitcast_fusion.4
  175.7 61.5 %all-reduce.12.cloned.1.call-done = f32[384,56]{0,1:T(8,128)} async-done(((f32[384,56]{0,1:T(8,128)}), f32[384,56]{0,1:T(8,128)}) %all-reduce.12.cloned.1.call-update) | async-done | bytes 86032
  237.9 56.2 %all_gather.23 = f32[24576,7]{0,1:T(8,128)S(1)} all-gather(f32[384,7]{0,1:T(8,128)S(1)} %fusion.18), channel_id=1, replica_groups=mesh['row'=64,'col'=8] {'row'}, dimensions={0}, use_global_device_ids=true | all-gather | bytes 698880 | tf_op jit(solution)/shard_map/all_gather | solution.py:20
  294.1 28.4 %all_to_all.96 = f32[8,3072,7]{1,2,0:T(8,128)S(1)} all-to-all(f32[8,3072,7]{1,2,0:T(8,128)S(1)} %bitcast.68), channel_id=1, replica_groups=mesh['row'=64,'col'=8] {'col'}, dimensions={0} | all-to-all | bytes 1376256 | tf_op jit(solution)/shard_map/all_to_all | solution.py:21
  322.6 7.4 convolution_bitcast_fusion.3
  330.1 64.8 %all-reduce.14.cloned.1.call-done = f32[384,56]{0,1:T(8,128)} async-done(((f32[384,56]{0,1:T(8,128)}), f32[384,56]{0,1:T(8,128)}) %all-reduce.14.cloned.1.call-update) | async-done | bytes 86032
  395.6 55.7 %all_gather.24 = f32[24576,7]{0,1:T(8,128)S(1)} all-gather(f32[384,7]{0,1:T(8,128)S(1)} %fusion.17), channel_id=1, replica_groups=mesh['row'=64,'col'=8] {'row'}, dimensions={0}, use_global_device_ids=true | all-gather | bytes 698880 | tf_op jit(solution)/shard_map/all_gather | solution.py:20
  451.4 28.6 %all_to_all.97 = f32[8,3072,7]{1,2,0:T(8,128)S(1)} all-to-all(f32[8,3072,7]{1,2,0:T(8,128)S(1)} %bitcast.69), channel_id=1, replica_groups=mesh['row'=64,'col'=8] {'col'}, dimensions={0} | all-to-all | bytes 1376256 | tf_op jit(solution)/shard_map/all_to_all | solution.py:21
  480.0 7.5 convolution_bitcast_fusion.2
  487.5 64.9 %all-reduce.16.cloned.1.call-done = f32[384,56]{0,1:T(8,128)} async-done(((f32[384,56]{0,1:T(8,128)}), f32[384,56]{0,1:T(8,128)}) %all-reduce.16.cloned.1.call-update) | async-done | bytes 86032
  553.2 55.7 %all_gather.25 = f32[24576,7]{0,1:T(8,128)S(1)} all-gather(f32[384,7]{0,1:T(8,128)S(1)} %fusion.14), channel_id=1, replica_groups=mesh['row'=64,'col'=8] {'row'}, dimensions={0}, use_global_device_ids=true | all-gather | bytes 698880 | tf_op jit(solution)/shard_map/all_gather | solution.py:20
  608.8 28.4 %all_to_all.98 = f32[8,3072,7]{1,2,0:T(8,128)S(1)} all-to-all(f32[8,3072,7]{1,2,0:T(8,128)S(1)} %bitcast.70), channel_id=1, replica_groups=mesh['row'=64,'col'=8] {'col'}, dimensions={0} | all-to-all | bytes 1376256 | tf_op jit(solution)/shard_map/all_to_all | solution.py:21
  637.3 7.5 convolution_bitcast_fusion.1
  644.8 64.9 %all-reduce.18.cloned.1.call-done = f32[384,56]{0,1:T(8,128)} async-done(((f32[384,56]{0,1:T(8,128)}), f32[384,56]{0,1:T(8,128)}) %all-reduce.18.cloned.1.call-update) | async-done | bytes 86032
  710.4 60.3 %all_gather.27 = f32[24576,7]{0,1:T(8,128)} all-gather(f32[384,7]{0,1:T(8,128)S(1)} %fusion.11), channel_id=1, replica_groups=mesh['row'=64,'col'=8] {'row'}, dimensions={0}, use_global_device_ids=true | all-gather | bytes 698880 | tf_op jit(solution)/shard_map/all_gather | solution.py:20
  775.8 33.0 %all-gather = f32[8,7,384]{2,1,0:T(8,128)S(1)} all-gather(f32[1,7,384]{2,1,0:T(8,128)S(1)} %bitcast.71), channel_id=1, replica_groups=mesh['row'=64,'col'=8] {'col'}, dimensions={0}, use_global_device_ids=true | all-gather | bytes 96768 | tf_op jit(solution)/shard_map/all_gather | solution.py:32
  808.9 7.4 convolution_bitcast_fusion
  816.7 74.4 %all-reduce.20.cloned.1.call-done = f32[384,56]{0,1:T(8,128)} async-done(((f32[384,56]{0,1:T(8,128)}), f32[384,56]{0,1:T(8,128)}) %all-reduce.20.cloned.1.call-update) | async-done | bytes 86032
  892.4 102.7 %all-reduce.5 = (f32[56,56]{1,0:T(8,128)S(1)}, f32[56,56]{1,0:T(8,128)S(1)}) all-reduce(f32[56,56]{1,0:T(8,128)S(1)} %dynamic_update_slice.6, f32[56,56]{1,0:T(8,128)S(1)} %dynamic_update_slice.7), channel_id=1, replica_groups=mesh['row'=64,'col'=8] {'row','col'}, use_global_device_ids=true, to_apply=%region_4.5 | all-reduce | flops 6272 | bytes 50176 | tf_op jit(solution)/shard_map/psum | solution.py:36
  995.2 5.1 cholesky.16
  (46 shorter events, 21.8 us)
Async XLA Ops:
  7.2 230.0 %all-reduce.12.cloned.1.call-start = ((), (), s32[]{:S(2)}) async-start(), calls=%async_computation.5 | async-start | bytes 172032
  172.4 222.5 %all-reduce.14.cloned.1.call-start = ((), (), s32[]{:S(2)}) async-start(), calls=%async_computation.6 | async-start | bytes 172032
  330.0 222.4 %all-reduce.16.cloned.1.call-start = ((), (), s32[]{:S(2)}) async-start(), calls=%async_computation.7 | async-start | bytes 172032
  487.5 222.2 %all-reduce.18.cloned.1.call-start = ((), (), s32[]{:S(2)}) async-start(), calls=%async_computation.8 | async-start | bytes 172032
  770.7 38.1 %all-to-all-start.4 = ((f32[8,3072,7]{1,2,0:T(8,128)}), f32[8,3072,7]{1,2,0:T(8,128)S(1)}, u32[]{:S(2)}, u32[]{:S(2)}) async-start(f32[8,3072,7]{1,2,0:T(8,128)} %bitcast.19), calls=%async_computation.4 | async-start | bytes 1572864 | tf_op jit(solution)/shard_map/all_to_all | solution.py:21
  775.8 115.3 %all-reduce.20.cloned.1.call-start = ((), (), s32[]{:S(2)}) async-start(), calls=%async_computation.9 | async-start | bytes 172032
Sparse Core Ops, SparseCore 0:
  172.5 64.5 all-reduce.11
  330.2 64.6 all-reduce.13
  487.6 64.7 all-reduce.15
  644.9 64.7 all-reduce.17
  816.5 74.5 all-reduce.19
where the time goes:
time: 1020 us; the launch traced here: 1010 us
  blocking collectives  598 us (59%)
  waiting for transfers between devices  330 us (32%)
  matrix products  40.4 us (4%)
  between operations  16.1 us (2%)
  other arithmetic  15.1 us (1%)
    unnamed x10, waiting for transfers between devices  330 us
    all_gather x5, blocking collectives, operate_on(): spread_rows = lax.all_gather(vectors, 'row', axis=0, tiled=True)  277 us
    all_to_all x4, blocking collectives, operate_on(): lax.all_to_all(spread_rows, 'col', split_axis=0, concat_axis=1, tiled=True)  116 us
    psum x1, blocking collectives, body(): gram_total = lax.psum(gram_part, ('row', 'col'))  103 us
    all_gather x1, blocking collectives, body(): spread = lax.all_gather(previous, 'row', axis=0, tiled=True)  70.1 us
    dot_general x5, matrix products, operate_on(): partial_sum = jnp.dot(hamiltonian, wanted, precision=lax.Precision.HIGHEST)  37.2 us
    all_gather x1, blocking collectives, body(): full_rows = lax.all_gather(current, 'col', axis=1, tiled=True)  33 us
  transfers between devices with their start and end apart: 6, of which 5 were waited for; matrix products, arithmetic and copies ran while one was open for 0% of the time, Pallas kernels for 0%

commit v1 on v0

--- a/solution.py
+++ b/solution.py
@@ -5,6 +5,19 @@
 
 N = 24576
 DEG = 4
+
+
+def register_the_pipes(q_in, mesh_ax):
+    wide_out = jnp.concatenate(
+        lax.all_to_all(
+            jnp.stack([q_in for _ in range(lax.psum(1, mesh_ax))]),
+            mesh_ax,
+            split_axis=0,
+            concat_axis=0,
+        ),
+        axis=0,
+    )
+    return wide_out
 
 
 def body(hamiltonian, previous, correlation_map, lower_cut, upper_bound):
@@ -17,7 +30,7 @@
     start_block = jnp.take(spread, correlation_map, axis=0)
 
     def operate_on(vectors):
-        spread_rows = lax.all_gather(vectors, "row", axis=0, tiled=True)
+        spread_rows = register_the_pipes(vectors, "row")
         wanted = lax.all_to_all(spread_rows, "col", split_axis=0, concat_axis=1, tiled=True)
         partial_sum = jnp.dot(hamiltonian, wanted, precision=lax.Precision.HIGHEST)
         return lax.psum_scatter(partial_sum, "col", scatter_dimension=1, tiled=True)

time: 1020 us -> 910 us (0.89)
  blocking collectives: 598 us -> 492 us
    all_gather x5 -> x0, blocking collectives: 277 us -> none  [operate_on(): spread_rows = lax.all_gather(vectors, 'row', axis=0, tiled=True)]
    all_to_all x0 -> x5, blocking collectives: none -> 177 us  [register_the_pipes(): lax.all_to_all(jnp.stack([q_in for _ in range(lax.psum(1, mesh_ax))]), me...]
where the time goes in v1:
time: 910 us; the launch traced here: 909 us
  blocking collectives  492 us (54%)
  waiting for transfers between devices  331 us (36%)
  matrix products  40.4 us (4%)
  between operations  15.9 us (2%)
  other arithmetic  15.1 us (2%)
  local copies, waits for them, and re-layouts  9.22 us (1%)
    unnamed x10, waiting for transfers between devices  331 us
    all_to_all x5, blocking collectives, register_the_pipes(): lax.all_to_all(jnp.stack([q_in for _ in range(lax.psum(1, mesh_ax))]), me...  177 us
    all_to_all x4, blocking collectives, operate_on(): lax.all_to_all(spread_rows, 'col', split_axis=0, concat_axis=1, tiled=True)  109 us
    psum x1, blocking collectives, body(): gram_total = lax.psum(gram_part, ('row', 'col'))  103 us
    all_gather x1, blocking collectives, body(): spread = lax.all_gather(previous, 'row', axis=0, tiled=True)  70.1 us
    dot_general x5, matrix products, operate_on(): partial_sum = jnp.dot(hamiltonian, wanted, precision=lax.Precision.HIGHEST)  37.2 us
    all_gather x1, blocking collectives, body(): full_rows = lax.all_gather(current, 'col', axis=1, tiled=True)  33 us
  transfers between devices with their start and end apart: 6, of which 5 were waited for; matrix products, arithmetic and copies ran while one was open for 0% of the time, Pallas kernels for 0%

profile of v1, /device:TPU:1, one launch (start us, length us, event | category | flops | bytes accessed | tf_op | source)
XLA Modules:
  0.0 908.5 jit_solution(9299446606013533600)
XLA Ops:
  9.4 70.1 %all_gather.6 = f32[24576,7]{1,0:T(8,128)} all-gather(f32[384,7]{1,0:T(8,128)S(1)} %copy.65), channel_id=1, replica_groups=mesh['row'=64,'col'=8] {'row'}, dimensions={0}, use_global_device_ids=true | all-gather | bytes 698880 | tf_op jit(solution)/shard_map/all_gather | solution.py:29
  79.6 5.7 gather_fusion
  85.5 27.3 %all_to_all.120 = f32[64,384,7]{1,2,0:T(8,128)S(1)} all-to-all(f32[64,384,7]{1,2,0:T(8,128)S(1)} %stack.10), channel_id=1, replica_groups=mesh['row'=64,'col'=8] {'row'}, dimensions={0} | all-to-all | bytes 1376256 | tf_op jit(solution)/shard_map/all_to_all | solution.py:12
  112.8 30.8 %all_to_all.121 = f32[8,3072,7]{1,2,0:T(8,128)S(1)} all-to-all(f32[8,3072,7]{1,2,0:T(8,128)S(1)} %bitcast.63), channel_id=1, replica_groups=mesh['row'=64,'col'=8] {'col'}, dimensions={0} | all-to-all | bytes 1376256 | tf_op jit(solution)/shard_map/all_to_all | solution.py:34
  143.7 7.4 convolution_bitcast_fusion.4
  154.4 62.1 %all-reduce.12.cloned.1.call-done = f32[384,56]{0,1:T(8,128)} async-done(((f32[384,56]{0,1:T(8,128)}), f32[384,56]{0,1:T(8,128)}) %all-reduce.12.cloned.1.call-update) | async-done | bytes 86032
  217.3 37.4 %all_to_all.122 = f32[64,384,7]{1,2,0:T(8,128)S(1)} all-to-all(f32[64,384,7]{1,2,0:T(8,128)S(1)} %stack.11), channel_id=1, replica_groups=mesh['row'=64,'col'=8] {'row'}, dimensions={0} | all-to-all | bytes 1376256 | tf_op jit(solution)/shard_map/all_to_all | solution.py:12
  254.7 26.1 %all_to_all.123 = f32[8,3072,7]{1,2,0:T(8,128)S(1)} all-to-all(f32[8,3072,7]{1,2,0:T(8,128)S(1)} %bitcast.65), channel_id=1, replica_groups=mesh['row'=64,'col'=8] {'col'}, dimensions={0} | all-to-all | bytes 1376256 | tf_op jit(solution)/shard_map/all_to_all | solution.py:34
  280.9 7.4 convolution_bitcast_fusion.3
  288.4 65.3 %all-reduce.14.cloned.1.call-done = f32[384,56]{0,1:T(8,128)} async-done(((f32[384,56]{0,1:T(8,128)}), f32[384,56]{0,1:T(8,128)}) %all-reduce.14.cloned.1.call-update) | async-done | bytes 86032
  354.5 37.4 %all_to_all.124 = f32[64,384,7]{1,2,0:T(8,128)S(1)} all-to-all(f32[64,384,7]{1,2,0:T(8,128)S(1)} %stack.12), channel_id=1, replica_groups=mesh['row'=64,'col'=8] {'row'}, dimensions={0} | all-to-all | bytes 1376256 | tf_op jit(solution)/shard_map/all_to_all | solution.py:12
  391.9 26.1 %all_to_all.125 = f32[8,3072,7]{1,2,0:T(8,128)S(1)} all-to-all(f32[8,3072,7]{1,2,0:T(8,128)S(1)} %bitcast.67), channel_id=1, replica_groups=mesh['row'=64,'col'=8] {'col'}, dimensions={0} | all-to-all | bytes 1376256 | tf_op jit(solution)/shard_map/all_to_all | solution.py:34
  418.0 7.5 convolution_bitcast_fusion.2
  425.6 65.3 %all-reduce.16.cloned.1.call-done = f32[384,56]{0,1:T(8,128)} async-done(((f32[384,56]{0,1:T(8,128)}), f32[384,56]{0,1:T(8,128)}) %all-reduce.16.cloned.1.call-update) | async-done | bytes 86032
  491.7 37.4 %all_to_all.126 = f32[64,384,7]{1,2,0:T(8,128)S(1)} all-to-all(f32[64,384,7]{1,2,0:T(8,128)S(1)} %stack.13), channel_id=1, replica_groups=mesh['row'=64,'col'=8] {'row'}, dimensions={0} | all-to-all | bytes 1376256 | tf_op jit(solution)/shard_map/all_to_all | solution.py:12
  529.1 26.1 %all_to_all.127 = f32[8,3072,7]{1,2,0:T(8,128)S(1)} all-to-all(f32[8,3072,7]{1,2,0:T(8,128)S(1)} %bitcast.69), channel_id=1, replica_groups=mesh['row'=64,'col'=8] {'col'}, dimensions={0} | all-to-all | bytes 1376256 | tf_op jit(solution)/shard_map/all_to_all | solution.py:34
  555.2 7.5 convolution_bitcast_fusion.1
  562.7 65.3 %all-reduce.18.cloned.1.call-done = f32[384,56]{0,1:T(8,128)} async-done(((f32[384,56]{0,1:T(8,128)}), f32[384,56]{0,1:T(8,128)}) %all-reduce.18.cloned.1.call-update) | async-done | bytes 86032
  628.9 37.5 %all_to_all.128 = f32[64,384,7]{1,2,0:T(8,128)} all-to-all(f32[64,384,7]{1,2,0:T(8,128)S(1)} %stack.14), channel_id=1, replica_groups=mesh['row'=64,'col'=8] {'row'}, dimensions={0} | all-to-all | bytes 1376256 | tf_op jit(solution)/shard_map/all_to_all | solution.py:12
  671.5 33.0 %all-gather = f32[8,7,384]{2,1,0:T(8,128)S(1)} all-gather(f32[1,7,384]{2,1,0:T(8,128)S(1)} %bitcast.71), channel_id=1, replica_groups=mesh['row'=64,'col'=8] {'col'}, dimensions={0}, use_global_device_ids=true | all-gather | bytes 96768 | tf_op jit(solution)/shard_map/all_gather | solution.py:45
  704.7 7.4 convolution_bitcast_fusion
  712.4 72.4 %all-reduce.20.cloned.1.call-done = f32[384,56]{0,1:T(8,128)} async-done(((f32[384,56]{0,1:T(8,128)}), f32[384,56]{0,1:T(8,128)}) %all-reduce.20.cloned.1.call-update) | async-done | bytes 86032
  786.2 102.9 %all-reduce.5 = (f32[56,56]{1,0:T(8,128)S(1)}, f32[56,56]{1,0:T(8,128)S(1)}) all-reduce(f32[56,56]{1,0:T(8,128)S(1)} %dynamic_update_slice.6, f32[56,56]{1,0:T(8,128)S(1)} %dynamic_update_slice.7), channel_id=1, replica_groups=mesh['row'=64,'col'=8] {'row','col'}, use_global_device_ids=true, to_apply=%region_4.5 | all-reduce | flops 6272 | bytes 50176 | tf_op jit(solution)/shard_map/psum | solution.py:49
  889.2 5.1 cholesky.16
  (51 shorter events, 22.0 us)
Async XLA Ops:
  7.2 209.3 %all-reduce.12.cloned.1.call-start = ((), (), s32[]{:S(2)}) async-start(), calls=%async_computation.10 | async-start | bytes 172032
  151.2 202.5 %all-reduce.14.cloned.1.call-start = ((), (), s32[]{:S(2)}) async-start(), calls=%async_computation.11 | async-start | bytes 172032
  288.3 202.6 %all-reduce.16.cloned.1.call-start = ((), (), s32[]{:S(2)}) async-start(), calls=%async_computation.12 | async-start | bytes 172032
  425.5 202.6 %all-reduce.18.cloned.1.call-start = ((), (), s32[]{:S(2)}) async-start(), calls=%async_computation.13 | async-start | bytes 172032
  666.3 38.2 %all-to-all-start.9 = ((f32[8,3072,7]{1,2,0:T(8,128)}), f32[8,3072,7]{1,2,0:T(8,128)S(1)}, u32[]{:S(2)}, u32[]{:S(2)}) async-start(f32[8,3072,7]{1,2,0:T(8,128)} %bitcast.19), calls=%async_computation.9 | async-start | bytes 1572864 | tf_op jit(solution)/shard_map/all_to_all | solution.py:34
  671.4 113.4 %all-reduce.20.cloned.1.call-start = ((), (), s32[]{:S(2)}) async-start(), calls=%async_computation.14 | async-start | bytes 172032
Sparse Core Ops, SparseCore 0:
  151.3 65.1 all-reduce.11
  288.4 65.1 all-reduce.13
  425.6 65.2 all-reduce.15
  562.8 65.1 all-reduce.17
  712.2 72.5 all-reduce.19
